TPU v7x, 1024 devices: a whole 8x8x8 slice. The times are simulated.
1024 devices in a mesh: section: 32 (over x_hi, z), dp: 32 (over x_lo, y, core).
Axes of the slice: x: 8 (x_hi: 4, x_lo: 2; x = x_hi * 2 + x_lo), y: 8, z: 8, core: 2. Of those that a mesh axis runs over, the one named last changes fastest.
Arguments:
- queries: bfloat16 [32, 12288, 1024], P('section', 'dp'), may hold values from -600 to 600
- images: bfloat16 [32, 128, 8192], P('dp', 'section'), may hold values from -6 to 6
- w_key: bfloat16 [32, 8192, 128], P('section', 'dp'), may hold values from -0.0625 to 0.0625
- w_value: bfloat16 [32, 8192, 128], P('section', 'dp'), may hold values from -0.0625 to 0.0625
- key_gain: float32 [8, 128], replicated, may hold values from 0.1 to 1.9
- d_out: bfloat16 [32, 12288, 1024], P('section', 'dp'), may hold values from -6 to 6
- img_len: int32 [32], P('dp'), may hold values from 32 to 128, as said below
- text_start: int32 [32], P('dp'), may hold values from 0 to 191
Outputs:
- attended: bfloat16 [32, 12288, 1024], P('section', 'dp')
- d_images: float32 [32, 128, 8192], P('dp', 'section')
Inputs may be any that keep to these rules, and one draw needn't show every extreme that they name: `img_len`: each sample uses a whole number of tiles of 32 tokens, 1 to 4 tiles; some sample uses all 4.
All inputs are finite; a program needn't handle non-finite values.
Results may differ from a plain program's by a relative error of at most 0.025.
Values may be sent and summed in bfloat16 or wider, within the bound.
No kernel may reach another device: no remote copies, remote signals or barrier semaphores. Data moves between devices by JAX's collectives and lax.ppermute only.
A program may use at most 32 MiB of HBM per device.

v0:
```python
import math

import jax
import jax.numpy as jnp
from jax import lax
from jax.sharding import PartitionSpec as P

KVH = 4


def attend(key_raw, value_raw, key_gain, queries, length, start):
    inverse = lax.rsqrt(jnp.mean(key_raw * key_raw, axis=-1, keepdims=True) + 1e-05)
    keys = (key_raw * inverse * key_gain).astype(jnp.bfloat16)
    values = value_raw.astype(jnp.bfloat16)
    head_size = key_gain.shape[-1]
    heads = queries.reshape(queries.shape[0], -1, head_size).astype(jnp.float32)
    scores = jnp.einsum("thd,jd->htj", heads, keys.astype(jnp.float32)) / math.sqrt(head_size)
    usable = jnp.arange(keys.shape[0]) < length
    scores = jnp.where(usable, scores, -1e30)
    scores = scores - jnp.max(scores, axis=-1, keepdims=True)
    expo = jnp.exp(scores)
    probs = (expo / jnp.sum(expo, axis=-1, keepdims=True)).astype(jnp.bfloat16)
    mixed = jnp.einsum("htj,jd->thd", probs.astype(jnp.float32), values.astype(jnp.float32))
    mixed = mixed.reshape(queries.shape[0], -1)
    shown = jnp.arange(queries.shape[0]) >= start
    return jnp.where(shown[:, None], mixed, 0.0)


def local(queries, images, w_key, w_value, key_gain, d_out, img_len, text_start):
    image_full = lax.all_gather(images[0], "section", axis=0, tiled=True)
    key_part = w_key[0]
    value_part = w_value[0]
    layer = lax.axis_index("section") // KVH
    gain = lax.dynamic_index_in_dim(key_gain, layer, 0, keepdims=False)
    key_weight, value_weight = (
        lax.all_gather(key_part, "dp", axis=0, tiled=True),
        lax.all_gather(value_part, "dp", axis=0, tiled=True),
    )
    key_raw = jnp.dot(image_full, key_weight, preferred_element_type=jnp.float32)
    value_raw = jnp.dot(image_full, value_weight, preferred_element_type=jnp.float32)
    query_rows = queries[0]
    length = img_len[0]
    start_row = text_start[0]
    mixed, pull_back = jax.vjp(
        lambda kr, vr: attend(kr, vr, gain, query_rows, length, start_row), key_raw, value_raw
    )
    d_key, d_value = pull_back(d_out[0].astype(jnp.float32))
    d_key_half = d_key.astype(jnp.bfloat16)
    d_value_half = d_value.astype(jnp.bfloat16)
    term = jnp.dot(d_key_half, key_weight.T, preferred_element_type=jnp.float32)
    own_grads = lax.psum_scatter(
        (term + jnp.dot(d_value_half, value_weight.T, preferred_element_type=jnp.float32)).astype(
            jnp.bfloat16
        ),
        "section",
        scatter_dimension=0,
        tiled=True,
    ).astype(jnp.float32)
    return (mixed.astype(jnp.bfloat16)[None], own_grads[None])


def solution(mesh):
    return jax.shard_map(
        local,
        mesh=mesh,
        in_specs=(
            P("section", "dp", None),
            P("dp", "section", None),
            P("section", "dp", None),
            P("section", "dp", None),
            P(),
            P("section", "dp", None),
            P("dp"),
            P("dp"),
        ),
        out_specs=(P("section", "dp", None), P("dp", "section", None)),
        check_vma=False,
    )
```

profile of v0, /device:TPU:64, one launch (start us, length us, event | category | flops | bytes accessed | tf_op | source)
XLA Modules:
  0.0 632.3 jit_solution(1990416275195523123)
XLA Ops:
  7.2 0.0 copy-start
  7.2 0.0 copy-start.2
  7.2 0.0 all-gather.7.cloned.1.call-start
  7.2 1.7 copy.25
  8.9 0.0 all-gather.7.cloned.1.call-update
  8.9 0.0 all-gather.11.cloned.1.call-start
  9.0 0.7 all-gather.11.cloned.1.call-update
  9.7 0.0 all-gather.9.cloned.1.call-start
  9.7 0.7 all-gather.9.cloned.1.call-update
  10.4 0.0 all-reduce.3.cloned.1.call-start
  10.5 1.5 copy.40
  13.3 0.0 copy-done.2
  13.3 0.4 copy.38
  13.7 0.0 copy-done
  13.7 119.3 %all-gather.7.cloned.1.call-done = bf16[1,128,8192]{2,0,1:T(2,128)(2,1)} async-done(((bf16[1,4,8192]{2,0,1:T(2,128)(2,1)}), bf16[1,128,8192]{2,0,1:T(2,128)(2,1)}) %all-gather.7.cloned.1.call-update) | async-done | bytes 2097168 | tf_op jit(solution)/shard_map/all_gather | solution.py:30
  133.0 65.6 %all-gather.11.cloned.1.call-done = bf16[1,8192,128]{2,1,0:T(8,128)(2,1)} async-done(((bf16[1,256,128]{2,1,0:T(8,128)(2,1)}), bf16[1,8192,128]{2,1,0:T(8,128)(2,1)}) %all-gather.11.cloned.1.call-update) | async-done | bytes 2097168 | tf_op jit(solution)/shard_map/all_gather | solution.py:36
  198.6 5.5 multiply_reduce_fusion.1
  204.2 0.5 bitcast_reduce_fusion
  204.7 0.2 fusion.64
  204.9 66.7 %all-gather.9.cloned.1.call-done = bf16[1,8192,128]{2,1,0:T(8,128)(2,1)} async-done(((bf16[1,256,128]{2,1,0:T(8,128)(2,1)}), bf16[1,8192,128]{2,1,0:T(8,128)(2,1)}) %all-gather.9.cloned.1.call-update) | async-done | bytes 2097168 | tf_op jit(solution)/shard_map/all_gather | solution.py:37
  271.6 5.3 fusion.57
  276.9 0.5 fusion.17
  277.5 0.6 fusion.25
  278.1 0.0 copy-start.1
  278.1 0.9 multiply_reduce_fusion
  279.1 0.6 copy-done.1
  279.7 2.7 fusion.5
  282.4 5.6 fusion
  288.0 0.0 all-reduce.3.cloned.1.call-update
  288.0 1.3 dynamic-slice
  289.9 0.5 fusion.94
  290.4 0.3 copy.30
  290.7 1.1 select_convert_fusion
  291.8 332.4 %all-reduce.3.cloned.1.call-done = bf16[128,8192]{1,0:T(8,128)(2,1)} async-done(((bf16[128,8192]{1,0:T(8,128)(2,1)}), bf16[128,8192]{1,0:T(8,128)(2,1)}) %all-reduce.3.cloned.1.call-update) | async-done | bytes 2097168
  624.2 1.6 bitcast_convert_fusion
  (8 shorter events, 0.1 us)
Async XLA Ops:
  7.2 6.5 %copy-start = (f32[8,128]{1,0:T(8,128)S(1)}, f32[8,128]{1,0:T(8,128)}, u32[]{:S(2)}) copy-start(f32[8,128]{1,0:T(8,128)} %param.12) | copy-start | bytes 12292
  7.2 6.1 copy-start.2
  7.2 125.8 %all-gather.7.cloned.1.call-start = ((), (), s32[]{:S(2)}) async-start(), calls=%async_computation | async-start | bytes 4325376 | tf_op jit(solution)/shard_map/all_gather | solution.py:30
  8.9 189.7 %all-gather.11.cloned.1.call-start = ((), (), s32[]{:S(2)}) async-start(), calls=%async_computation.2 | async-start | bytes 2162688 | tf_op jit(solution)/shard_map/all_gather | solution.py:36
  9.7 261.9 %all-gather.9.cloned.1.call-start = ((), (), s32[]{:S(2)}) async-start(), calls=%async_computation.1 | async-start | bytes 2162688 | tf_op jit(solution)/shard_map/all_gather | solution.py:37
  10.4 613.8 %all-reduce.3.cloned.1.call-start = ((), (), s32[]{:S(2)}) async-start(), calls=%async_computation.3 | async-start | bytes 4194304
  278.1 1.6 copy-start.1
Sparse Core Ops, SparseCore 0:
  12.9 120.0 all-gather.6
  135.7 62.8 all-gather.10
  201.4 70.1 all-gather.8
  288.1 336.0 all-reduce.2
where the time goes:
time: 633 us; the launch traced here: 632 us
  waiting for transfers between devices  585 us (92%)
  matrix products  21.5 us (3%)
  between operations  15.9 us (3%)
    unnamed x5, waiting for transfers between devices  334 us
    all_gather x1, waiting for transfers between devices, local(): image_full = lax.all_gather(images[0], 'section', axis=0, tiled=True)  119 us
    all_gather x1, waiting for transfers between devices, local(): lax.all_gather(value_part, 'dp', axis=0, tiled=True)  66.7 us
    all_gather x1, waiting for transfers between devices, local(): lax.all_gather(key_part, 'dp', axis=0, tiled=True)  65.6 us
  transfers between devices with their start and end apart: 4, of which 4 were waited for; matrix products, arithmetic and copies ran while one was open for 2% of the time, Pallas kernels for 0%

commit v1 on v0

v1 whole, which is shorter than its diff:
```python
import math

import jax
import jax.numpy as jnp
from jax import lax
from jax.sharding import Mesh
from jax.sharding import PartitionSpec as P

KVH = 4
PAIR = 2
SECTION = ("rest", "pair")
DP = ("xl", "y", "c")


def attend(key_raw, value_raw, key_gain, queries, length, start):
    inverse = lax.rsqrt(jnp.mean(key_raw * key_raw, axis=-1, keepdims=True) + 1e-05)
    keys = (key_raw * inverse * key_gain).astype(jnp.bfloat16)
    values = value_raw.astype(jnp.bfloat16)
    head_size = key_gain.shape[-1]
    heads = queries.reshape(queries.shape[0], -1, head_size).astype(jnp.float32)
    scores = jnp.einsum("thd,jd->htj", heads, keys.astype(jnp.float32)) / math.sqrt(head_size)
    usable = jnp.arange(keys.shape[0]) < length
    scores = jnp.where(usable, scores, -1e30)
    scores = scores - jnp.max(scores, axis=-1, keepdims=True)
    expo = jnp.exp(scores)
    probs = (expo / jnp.sum(expo, axis=-1, keepdims=True)).astype(jnp.bfloat16)
    mixed = jnp.einsum("htj,jd->thd", probs.astype(jnp.float32), values.astype(jnp.float32))
    mixed = mixed.reshape(queries.shape[0], -1)
    shown = jnp.arange(queries.shape[0]) >= start
    return jnp.where(shown[:, None], mixed, 0.0)


def local(queries, images, w_key, w_value, key_gain, d_out, img_len, text_start):
    rows, model = images.shape[1:]
    ny = lax.axis_size("y")
    nrest = lax.axis_size("rest")
    head = w_key.shape[-1]
    unit = w_key.shape[1] // PAIR
    nxc = lax.axis_size("xl") * lax.axis_size("c")
    own = jnp.concatenate([w_key[0], w_value[0]], axis=1).reshape(PAIR, 1, unit, 2 * head)
    own = jnp.broadcast_to(own, (PAIR, nxc, unit, 2 * head)).reshape(PAIR * nxc, unit, 2 * head)
    near = lax.all_to_all(own, ("pair", "xl", "c"), 0, 0)
    weight = lax.all_gather(near, "y", axis=0, tiled=True)
    weight = weight.reshape(ny, PAIR, nxc * unit, 2 * head)

    pieces = images[0].reshape(rows, 2, ny, 2, PAIR, unit).transpose(4, 2, 1, 3, 0, 5)
    pieces = pieces.reshape(PAIR, ny * nxc, rows, unit)
    halves = lax.all_to_all(pieces, "pair", 0, 0)
    mine = halves.transpose(1, 0, 2, 3).reshape(ny * nxc, PAIR * rows, unit)
    spread = jnp.broadcast_to(mine[None], (nrest,) + mine.shape)
    full = lax.all_to_all(spread, "rest", 0, 0)
    tokens = nrest * PAIR * rows
    image_half = full.transpose(0, 2, 1, 3).reshape(tokens, ny, nxc * unit)

    part = jnp.einsum("tyr,yhrn->htn", image_half, weight, preferred_element_type=jnp.float32)
    both = lax.all_to_all(part, "pair", 0, 0)
    raw = both[0] + both[1]

    layer = lax.axis_index(SECTION) // KVH
    gain = lax.dynamic_index_in_dim(key_gain, layer, 0, keepdims=False)
    mixed, pull_back = jax.vjp(
        lambda kr, vr: attend(kr, vr, gain, queries[0], img_len[0], text_start[0]),
        raw[:, :head],
        raw[:, head:],
    )
    d_key, d_value = pull_back(d_out[0].astype(jnp.float32))
    d_own = jnp.concatenate([d_key, d_value], axis=1).astype(jnp.bfloat16)
    d_both = lax.all_gather(d_own, "pair", axis=0)
    term = jnp.einsum("htn,yhrn->tyr", d_both, weight, preferred_element_type=jnp.float32)
    term = term.astype(jnp.bfloat16).reshape(nrest, PAIR * rows, model // PAIR)
    terms = lax.all_to_all(term, "rest", 0, 0)
    total = jnp.sum(terms.astype(jnp.float32), axis=0)
    total = total.reshape(PAIR, rows, model // PAIR)
    grads = lax.all_to_all(total, "pair", 0, 0)
    grads = grads.reshape(PAIR, rows, ny, 2, 2, unit).transpose(1, 3, 2, 4, 0, 5)
    return mixed.astype(jnp.bfloat16)[None], grads.reshape(1, rows, model)


def solution(mesh):
    sections, samples = mesh.shape["section"], mesh.shape["dp"]
    fine = Mesh(
        mesh.devices.reshape(sections // PAIR, PAIR, 2, samples // 4, 2), SECTION + DP
    )
    return jax.shard_map(
        local,
        mesh=fine,
        in_specs=(
            P(SECTION, DP, None),
            P(DP, SECTION, None),
            P(SECTION, DP, None),
            P(SECTION, DP, None),
            P(),
            P(SECTION, DP, None),
            P(DP),
            P(DP),
        ),
        out_specs=(P(SECTION, DP, None), P(DP, SECTION, None)),
        check_vma=False,
    )
```

time: 633 us -> 189 us (0.30)
  the two profiles are of different devices: /device:TPU:64 before, /device:TPU:60 now
where the time goes in v1:
time: 189 us; the launch traced here: 188 us
  waiting for transfers between devices  83.7 us (44%)
  starting transfers between devices  40.6 us (21%)
  blocking collectives  25.6 us (14%)
  between operations  15.6 us (8%)
  matrix products  11.5 us (6%)
  local copies, waits for them, and re-layouts  7.93 us (4%)
  other arithmetic  3.11 us (2%)
    all_to_all x1, waiting for transfers between devices, local(): terms = lax.all_to_all(term, 'rest', 0, 0)  38 us
    all_to_all x1, waiting for transfers between devices, local(): full = lax.all_to_all(spread, 'rest', 0, 0)  27.3 us
    all_to_all x1, starting transfers between devices, local(): full = lax.all_to_all(spread, 'rest', 0, 0)  20.2 us
    all_to_all x1, blocking collectives, local(): near = lax.all_to_all(own, ('pair', 'xl', 'c'), 0, 0)  14.2 us
    all_to_all x1, starting transfers between devices, local(): terms = lax.all_to_all(term, 'rest', 0, 0)  13.4 us
    all_gather x1, waiting for transfers between devices, local(): weight = lax.all_gather(near, 'y', axis=0, tiled=True)  11.9 us
    all_to_all x1, blocking collectives, local(): halves = lax.all_to_all(pieces, 'pair', 0, 0)  6.5 us
    all_gather x1, blocking collectives, local(): d_both = lax.all_gather(d_own, 'pair', axis=0)  4.93 us
  transfers between devices with their start and end apart: 5, of which 5 were waited for; matrix products, arithmetic and copies ran while one was open for 3% of the time, Pallas kernels for 0%

profile of v1, /device:TPU:60, one launch (start us, length us, event | category | flops | bytes accessed | tf_op | source)
XLA Modules:
  0.0 188.0 jit_solution(14023116941367917092)
XLA Ops:
  7.2 0.0 copy-start
  7.2 0.0 copy-start.5
  7.2 0.0 all-gather.2.cloned.1.call-start
  7.2 0.9 maximum_bitcast_fusion
  8.2 14.2 %all_to_all.30 = bf16[8,128,256]{2,1,0:T(8,128)(2,1)} all-to-all(bf16[8,128,256]{2,1,0:T(8,128)(2,1)S(1)} %bitcast.143), channel_id=1, replica_groups=mesh['rest'=16,'pair'=2,'xl'=2,'y'=8,'c'=2] {'pair','xl','c'}, dimensions={0} | all-to-all | bytes 1048576 | tf_op jit(solution)/shard_map/all_to_all | solution.py:42
  22.4 0.0 all-gather.2.cloned.1.call-update
  22.4 0.0 copy-done.5
  22.4 0.1 reshape_squeeze.3
  22.5 6.5 %all_to_all.31 = bf16[2,32,4,128]{3,1,2,0:T(8,128)(2,1)S(1)} all-to-all(bf16[2,32,4,128]{3,1,2,0:T(8,128)(2,1)S(1)} %bitcast.150), channel_id=1, replica_groups=mesh['rest'=16,'pair'=2,'xl'=2,'y'=8,'c'=2] {'pair'}, dimensions={0} | all-to-all | bytes 131072 | tf_op jit(solution)/shard_map/all_to_all | solution.py:48
  29.0 1.2 broadcast_in_dim.66
  30.2 20.2 %all-to-all-start.2 = ((bf16[16,32,8,128]{3,1,2,0:T(8,128)(2,1)}), bf16[16,32,8,128]{3,1,2,0:T(8,128)(2,1)S(1)}, u32[]{:S(2)}, u32[]{:S(2)}) async-start(bf16[16,32,8,128]{3,1,2,0:T(8,128)(2,1)} %broadcast_in_dim.66), calls=%async_computation.2 | async-start | bytes 2097152 | tf_op jit(solution)/shard_map/all_to_all | solution.py:51
  51.1 27.3 %all-to-all-done.2 = bf16[16,32,8,128]{3,1,2,0:T(8,128)(2,1)S(1)} async-done(((bf16[16,32,8,128]{3,1,2,0:T(8,128)(2,1)}), bf16[16,32,8,128]{3,1,2,0:T(8,128)(2,1)S(1)}, u32[]{:S(2)}, u32[]{:S(2)}) %all-to-all-start.2) | async-done | bytes 1048608 | tf_op jit(solution)/shard_map/all_to_all | solution.py:51
  78.4 0.6 reshape.149
  79.0 11.9 %all-gather.2.cloned.1.call-done = bf16[64,128,256]{2,1,0:T(8,128)(2,1)} async-done(((bf16[8,128,256]{2,1,0:T(8,128)(2,1)}), bf16[64,128,256]{2,1,0:T(8,128)(2,1)}) %all-gather.2.cloned.1.call-update) | async-done | bytes 4194320 | tf_op jit(solution)/shard_map/all_gather | solution.py:43
  90.9 0.0 copy-start.1
  90.9 4.3 %convolution_bitcast_fusion = f32[2,128,256]{1,2,0:T(8,128)} fusion(bf16[8,2,512,256]{3,2,1,0:T(8,128)(2,1)} %bitcast.138, bf16[128,8,512,1]{2,1,0,3:T(8,128)(2,1)S(1)} %bitcast.144), kind=kOutput, calls=%fused_computation.33 | convolution fusion | flops 536870912 | bytes 5505024 | tf_op jit(solution)/shard_map/tyr,yhrn->htn/dot_general | solution.py:55
  95.2 0.0 copy-start.2
  95.2 3.6 %all-to-all-start.3 = ((f32[2,128,256]{1,2,0:T(8,128)}), f32[2,128,256]{1,2,0:T(8,128)S(1)}, u32[]{:S(2)}, u32[]{:S(2)}) async-start(f32[2,128,256]{1,2,0:T(8,128)} %convolution_bitcast_fusion), calls=%async_computation.3 | async-start | bytes 524288 | tf_op jit(solution)/shard_map/all_to_all | solution.py:56
  98.8 0.0 copy-start.6
  99.5 0.0 copy-done.1
  99.5 0.4 copy.73
  99.8 0.0 copy-done.2
  99.8 1.2 copy.71
  101.0 0.0 copy-done
  101.0 3.1 %all-to-all-done.3 = f32[2,128,256]{1,2,0:T(8,128)S(1)} async-done(((f32[2,128,256]{1,2,0:T(8,128)}), f32[2,128,256]{1,2,0:T(8,128)S(1)}, u32[]{:S(2)}, u32[]{:S(2)}) %all-to-all-start.3) | async-done | bytes 262176 | tf_op jit(solution)/shard_map/all_to_all | solution.py:56
  104.2 0.0 copy-start.3
  104.2 0.5 bitcast_reduce_fusion
  104.7 0.2 fusion.46
  104.9 0.0 copy-start.4
  104.9 0.4 copy-done.3
  105.3 0.4 fusion.42
  105.7 0.0 copy-done.6
  105.7 0.6 fusion.7
  106.3 0.6 fusion.15
  107.0 0.0 copy-done.4
  107.0 0.9 multiply_reduce_fusion
  108.0 0.1 copy.58
  108.1 4.9 %all_gather.8 = bf16[2,128,256]{2,1,0:T(8,128)(2,1)S(1)} all-gather(bf16[1,128,256]{2,1,0:T(8,128)(2,1)S(1)} %copy.58), channel_id=1, replica_groups=mesh['rest'=16,'pair'=2,'xl'=2,'y'=8,'c'=2] {'pair'}, dimensions={0}, use_global_device_ids=true | all-gather | bytes 196608 | tf_op jit(solution)/shard_map/all_gather | solution.py:68
  113.0 3.7 %bitcast_convert_fusion = bf16[128,8,512]{2,0,1:T(8,128)(2,1)S(1)} fusion(bf16[8,2,512,256]{3,2,1,0:T(8,128)(2,1)} %bitcast.139, bf16[2,128,256]{2,1,0:T(8,128)(2,1)S(1)} %all_gather.8), kind=kOutput, calls=%fused_computation.3 | convolution fusion | flops 537395200 | bytes 5373952 | tf_op jit(solution)/shard_map/htn,yhrn->tyr/dot_general | solution.py:69
  116.7 0.6 copy.59
  117.3 1.3 reshape.151
  118.6 13.4 %all-to-all-start.4 = ((bf16[16,8,4096]{2,1,0:T(8,128)(2,1)}), bf16[16,8,4096]{2,1,0:T(8,128)(2,1)S(1)}, u32[]{:S(2)}, u32[]{:S(2)}) async-start(bf16[16,8,4096]{2,1,0:T(8,128)(2,1)} %reshape.151), calls=%async_computation.4 | async-start | bytes 2097152 | tf_op jit(solution)/shard_map/all_to_all | solution.py:71
  132.0 1.1 fusion.68
  133.2 0.0 copy-start.7
  133.2 0.3 copy.53
  133.5 38.0 %all-to-all-done.4 = bf16[16,8,4096]{2,1,0:T(8,128)(2,1)S(1)} async-done(((bf16[16,8,4096]{2,1,0:T(8,128)(2,1)}), bf16[16,8,4096]{2,1,0:T(8,128)(2,1)S(1)}, u32[]{:S(2)}, u32[]{:S(2)}) %all-to-all-start.4) | async-done | bytes 1048608 | tf_op jit(solution)/shard_map/all_to_all | solution.py:71
  171.5 0.1 convert_reduce_fusion
  171.6 0.7 reshape.152
  172.3 3.4 %all-to-all-start.5 = ((f32[2,4,4096]{2,1,0:T(4,128)}), f32[2,4,4096]{2,1,0:T(4,128)S(1)}, u32[]{:S(2)}, u32[]{:S(2)}) async-start(f32[2,4,4096]{2,1,0:T(4,128)} %reshape.152), calls=%async_computation.5 | async-start | bytes 262144 | tf_op jit(solution)/shard_map/all_to_all | solution.py:74
  175.7 0.0 copy-done.7
  175.7 1.1 select_convert_fusion
  176.8 3.4 %all-to-all-done.5 = f32[2,4,4096]{2,1,0:T(4,128)S(1)} async-done(((f32[2,4,4096]{2,1,0:T(4,128)}), f32[2,4,4096]{2,1,0:T(4,128)S(1)}, u32[]{:S(2)}, u32[]{:S(2)}) %all-to-all-start.5) | async-done | bytes 131104 | tf_op jit(solution)/shard_map/all_to_all | solution.py:74
  180.2 0.1 reshape.153
  180.3 0.1 copy.60
  180.4 0.8 reshape.154
  (14 shorter events, 0.2 us)
Async XLA Ops:
  7.2 93.8 %copy-start = (f32[8,128]{1,0:T(8,128)S(1)}, f32[8,128]{1,0:T(8,128)}, u32[]{:S(2)}) copy-start(f32[8,128]{1,0:T(8,128)} %param.12) | copy-start | bytes 12292
  7.2 15.2 %copy-start.5 = (bf16[1,4,8192]{2,1,0:T(4,128)(2,1)S(1)}, bf16[1,4,8192]{2,1,0:T(4,128)(2,1)}, u32[]{:S(2)}) copy-start(bf16[1,4,8192]{2,1,0:T(4,128)(2,1)} %param.9) | copy-start | bytes 196612
  7.2 83.7 %all-gather.2.cloned.1.call-start = ((), (), s32[]{:S(2)}) async-start(), calls=%async_computation.6 | async-start | bytes 4718592 | tf_op jit(solution)/shard_map/all_gather | solution.py:43
  30.2 48.2 %all-to-all-start.2 = ((bf16[16,32,8,128]{3,1,2,0:T(8,128)(2,1)}), bf16[16,32,8,128]{3,1,2,0:T(8,128)(2,1)S(1)}, u32[]{:S(2)}, u32[]{:S(2)}) async-start(bf16[16,32,8,128]{3,1,2,0:T(8,128)(2,1)} %broadcast_in_dim.66), calls=%async_computation.2 | async-start | bytes 2097152 | tf_op jit(solution)/shard_map/all_to_all | solution.py:51
  90.9 8.5 %copy-start.1 = (bf16[1,384,1024]{2,1,0:T(8,128)(2,1)S(1)}, bf16[1,384,1024]{2,1,0:T(8,128)(2,1)}, u32[]{:S(2)}) copy-start(bf16[1,384,1024]{2,1,0:T(8,128)(2,1)} %param.8) | copy-start | bytes 2359300
  95.2 4.6 %copy-start.2 = (bf16[1,384,1024]{2,1,0:T(8,128)(2,1)S(1)}, bf16[1,384,1024]{2,1,0:T(8,128)(2,1)}, u32[]{:S(2)}) copy-start(bf16[1,384,1024]{2,1,0:T(8,128)(2,1)} %param.13) | copy-start | bytes 2359300
  95.2 8.9 %all-to-all-start.3 = ((f32[2,128,256]{1,2,0:T(8,128)}), f32[2,128,256]{1,2,0:T(8,128)S(1)}, u32[]{:S(2)}, u32[]{:S(2)}) async-start(f32[2,128,256]{1,2,0:T(8,128)} %convolution_bitcast_fusion), calls=%async_computation.3 | async-start | bytes 524288 | tf_op jit(solution)/shard_map/all_to_all | solution.py:56
  98.8 7.0 %copy-start.6 = (pred[384]{0:T(512)(128)(4,1)}, pred[384]{0:T(512)(128)(4,1)S(1)}, u32[]{:S(2)}) copy-start(pred[384]{0:T(512)(128)(4,1)S(1)} %iota_compare_fusion) | copy-start | bytes 1156
  104.2 1.1 copy-start.3
  104.9 2.1 %copy-start.4 = (f32[8,384]{1,0:T(8,128)}, f32[8,384]{1,0:T(8,128)S(1)}, u32[]{:S(2)}) copy-start(f32[8,384]{1,0:T(8,128)S(1)} %fusion.46) | copy-start | bytes 36868
  118.6 52.9 %all-to-all-start.4 = ((bf16[16,8,4096]{2,1,0:T(8,128)(2,1)}), bf16[16,8,4096]{2,1,0:T(8,128)(2,1)S(1)}, u32[]{:S(2)}, u32[]{:S(2)}) async-start(bf16[16,8,4096]{2,1,0:T(8,128)(2,1)} %reshape.151), calls=%async_computation.4 | async-start | bytes 2097152 | tf_op jit(solution)/shard_map/all_to_all | solution.py:71
  133.2 42.5 %copy-start.7 = (pred[384]{0:T(512)(128)(4,1)S(1)}, pred[384]{0:T(512)(128)(4,1)}, u32[]{:S(2)}) copy-start(pred[384]{0:T(512)(128)(4,1)} %copy-done.6) | copy-start | bytes 1156
  172.3 7.8 %all-to-all-start.5 = ((f32[2,4,4096]{2,1,0:T(4,128)}), f32[2,4,4096]{2,1,0:T(4,128)S(1)}, u32[]{:S(2)}, u32[]{:S(2)}) async-start(f32[2,4,4096]{2,1,0:T(4,128)} %reshape.152), calls=%async_computation.5 | async-start | bytes 262144 | tf_op jit(solution)/shard_map/all_to_all | solution.py:74
Sparse Core Ops, SparseCore 0:
  22.5 68.3 all-gather.1

commit v2 on v1

v2 whole, which is shorter than its diff:
```python
import math

import jax
import jax.numpy as jnp
from jax import lax
from jax.sharding import Mesh
from jax.sharding import PartitionSpec as P


KVH = 4
QUAD = 4
REST = ("xh", "zh")
SECTION = REST + ("quad",)
DP = ("xl", "y", "c")


def attend(key_raw, value_raw, key_gain, queries, usable, start):
    inverse = lax.rsqrt(jnp.mean(key_raw * key_raw, axis=-1, keepdims=True) + 1e-05)
    keys = (key_raw * inverse * key_gain).astype(jnp.bfloat16)
    values = value_raw.astype(jnp.bfloat16)
    head_size = key_gain.shape[-1]
    heads = queries.reshape(queries.shape[0], -1, head_size).astype(jnp.float32)
    scores = jnp.einsum("thd,jd->htj", heads, keys.astype(jnp.float32)) / math.sqrt(head_size)
    scores = jnp.where(usable, scores, -1e30)
    scores = scores - jnp.max(scores, axis=-1, keepdims=True)
    expo = jnp.exp(scores)
    probs = (expo / jnp.sum(expo, axis=-1, keepdims=True)).astype(jnp.bfloat16)
    mixed = jnp.einsum("htj,jd->thd", probs.astype(jnp.float32), values.astype(jnp.float32))
    mixed = mixed.reshape(queries.shape[0], -1)
    shown = jnp.arange(queries.shape[0]) >= start
    return jnp.where(shown[:, None], mixed, 0.0)


def local(queries, images, w_key, w_value, key_gain, d_out, img_len, text_start):
    rows, model = images.shape[1:]
    ny, nrest = lax.axis_size("y"), lax.axis_size(REST)
    head = w_key.shape[-1]
    unit = w_key.shape[1] // QUAD
    wide = 2 * unit

    own = jnp.concatenate([w_key[0], w_value[0]], axis=1).reshape(QUAD, 1, unit, 2 * head)
    own = jnp.broadcast_to(own, (QUAD, 2, unit, 2 * head)).reshape(QUAD * 2, unit, 2 * head)
    near = lax.all_to_all(own, ("quad", "xl"), 0, 0)
    weight = lax.all_to_all(jnp.broadcast_to(near[None], (ny,) + near.shape), "y", 0, 0)
    weight = weight.reshape(ny, QUAD, wide, 2 * head)

    core = lax.axis_index("c")
    pieces = images[0].reshape(rows, 2, ny, 2, QUAD, unit).transpose(3, 4, 2, 0, 1, 5)
    pieces = pieces.reshape(2, QUAD, ny, rows, wide)
    pieces = lax.all_gather(pieces, "c", axis=0)
    pieces = lax.dynamic_index_in_dim(pieces, core, 1, keepdims=False)
    pieces = lax.all_gather(pieces, "quad", axis=0)
    pieces = lax.dynamic_index_in_dim(pieces, lax.axis_index("quad"), 2, keepdims=False)
    pieces = pieces.transpose(1, 2, 0, 3, 4).reshape(2, ny, QUAD * rows, wide)
    pieces = lax.all_gather(pieces, "zh", axis=0)
    image = lax.all_gather(pieces, "xh", axis=0)
    image = image.reshape((nrest,) + image.shape[2:])

    theirs = lax.dynamic_index_in_dim(image, 1 - core, 1, keepdims=False)
    part = jnp.einsum("zyrd,yhdn->hzrn", theirs, weight, preferred_element_type=jnp.float32)
    part = lax.ppermute(part, "c", [(0, 1), (1, 0)])
    mine = lax.dynamic_index_in_dim(image, core, 1, keepdims=False)
    part = part + jnp.einsum("zyrd,yhdn->hzrn", mine, weight, preferred_element_type=jnp.float32)
    part = part.reshape(QUAD, nrest * QUAD * rows, 2 * head)
    coarse = lax.reduce_precision(part[:, :, :head], 8, 7)
    part = jnp.concatenate([coarse, part[:, :, :head] - coarse, part[:, :, head:]], axis=2)
    part = lax.all_to_all(part.astype(jnp.bfloat16), "quad", 0, 0)
    part = jnp.sum(part.astype(jnp.float32), axis=0)
    key_raw = part[:, :head] + part[:, head : 2 * head]
    value_raw = part[:, 2 * head :]

    layer = lax.axis_index(SECTION) // KVH
    usable = jnp.arange(nrest * QUAD * rows) < img_len[0]
    gain = lax.dynamic_index_in_dim(key_gain, layer, 0, keepdims=False)
    mixed, pull_back = jax.vjp(
        lambda kr, vr: attend(kr, vr, gain, queries[0], usable, text_start[0]),
        key_raw,
        value_raw,
    )
    d_key, d_value = pull_back(d_out[0].astype(jnp.float32))
    d_own = jnp.concatenate([d_key, d_value], axis=1).astype(jnp.bfloat16)
    d_heads = lax.all_to_all(jnp.broadcast_to(d_own[None], (QUAD,) + d_own.shape), "quad", 0, 0)
    d_both = lax.all_gather(d_heads, "c", axis=0)

    d_both = d_both.reshape(2, QUAD, nrest, QUAD * rows, 2 * head)
    term = jnp.einsum("shzrn,yhdn->zsyrd", d_both, weight, preferred_element_type=jnp.float32)
    term = lax.all_to_all(term.astype(jnp.bfloat16), REST, 0, 0)
    total = jnp.sum(term.astype(jnp.float32), axis=0)
    total = total.reshape(2, ny, QUAD, rows, wide).transpose(2, 0, 1, 3, 4)
    total = total.reshape(QUAD * 2, ny, rows, wide)
    grads = lax.all_to_all(total, ("quad", "c"), 0, 0)
    grads = grads.reshape(QUAD, 2, ny, rows, 2, unit).transpose(3, 4, 2, 1, 0, 5)
    return mixed.astype(jnp.bfloat16)[None], grads.reshape(1, rows, model)


def solution(mesh):
    sections, samples = mesh.shape["section"], mesh.shape["dp"]
    fine = Mesh(mesh.devices.reshape(sections // (2 * QUAD), 2, QUAD, 2, samples // 4, 2), SECTION + DP)
    return jax.shard_map(
        local,
        mesh=fine,
        in_specs=(
            P(SECTION, DP, None),
            P(DP, SECTION, None),
            P(SECTION, DP, None),
            P(SECTION, DP, None),
            P(),
            P(SECTION, DP, None),
            P(DP),
            P(DP),
        ),
        out_specs=(P(SECTION, DP, None), P(DP, SECTION, None)),
        check_vma=False,
    )
```

time: 189 us -> 171 us (0.905)
  the two profiles are of different devices: /device:TPU:60 before, /device:TPU:2 now
where the time goes in v2:
time: 171 us; the launch traced here: 170 us
  blocking collectives  80.2 us (47%)
  waiting for transfers between devices  39.3 us (23%)
  starting transfers between devices  29.5 us (17%)
  local copies, waits for them, and re-layouts  7.71 us (5%)
  matrix products  6.96 us (4%)
  other arithmetic  3.93 us (2%)
  between operations  2.42 us (1%)
    all_to_all x1, blocking collectives, local(): near = lax.all_to_all(own, ('quad', 'xl'), 0, 0)  22.3 us
    all_to_all x1, waiting for transfers between devices, local(): term = lax.all_to_all(term.astype(jnp.bfloat16), REST, 0, 0)  17.7 us
    all_gather x1, blocking collectives, local(): image = lax.all_gather(pieces, 'xh', axis=0)  16.1 us
    all_to_all x1, starting transfers between devices, local(): term = lax.all_to_all(term.astype(jnp.bfloat16), REST, 0, 0)  15.2 us
    all_gather x1, blocking collectives, local(): pieces = lax.all_gather(pieces, 'quad', axis=0)  14 us
    all_gather x1, blocking collectives, local(): pieces = lax.all_gather(pieces, 'zh', axis=0)  12.9 us
    all_to_all x1, blocking collectives, local(): lax.all_to_all(jnp.broadcast_to(d_own[None], (QUAD,) + d_own.shape), 'qua...  10.8 us
    all_to_all x1, waiting for transfers between devices, local(): part = lax.all_to_all(part.astype(jnp.bfloat16), 'quad', 0, 0)  9.85 us
  transfers between devices with their start and end apart: 5, of which 5 were waited for; matrix products, arithmetic and copies ran while one was open for 3% of the time, Pallas kernels for 0%

profile of v2, /device:TPU:2, one launch (start us, length us, event | category | flops | bytes accessed | tf_op | source)
XLA Modules:
  0.0 170.0 jit_solution(12959924833497507861)
XLA Ops:
  0.6 0.0 copy-start
  0.6 0.9 maximum_bitcast_fusion
  1.6 22.3 %all_to_all.30 = bf16[8,64,256]{2,1,0:T(8,128)(2,1)S(1)} all-to-all(bf16[8,64,256]{2,1,0:T(8,128)(2,1)S(1)} %bitcast.173), channel_id=1, replica_groups=mesh['xh'=4,'zh'=2,'quad'=4,'xl'=2,'y'=8,'c'=2] {'quad','xl'}, dimensions={0} | all-to-all | bytes 524288 | tf_op jit(solution)/shard_map/all_to_all | solution.py:43
  23.9 1.6 broadcast_in_dim.70
  25.5 4.9 %all-to-all-start.1 = ((bf16[8,8,64,256]{3,2,1,0:T(8,128)(2,1)}), bf16[8,8,64,256]{3,2,1,0:T(8,128)(2,1)S(1)}, u32[]{:S(2)}, u32[]{:S(2)}) async-start(bf16[8,8,64,256]{3,2,1,0:T(8,128)(2,1)} %broadcast_in_dim.70), calls=%async_computation.1 | async-start | bytes 4194304 | tf_op jit(solution)/shard_map/all_to_all | solution.py:44
  30.4 0.2 reshape_squeeze.3
  30.6 0.1 copy.126
  30.7 0.1 all_gather_reshape.6
  30.9 1.9 %all_gather.24 = bf16[2,2,4,8,4,128]{5,3,4,2,1,0:T(8,128)(2,1)S(1)} all-gather(bf16[1,2,4,8,4,128]{5,3,4,2,1,0:T(8,128)(2,1)S(1)} %all_gather_reshape.6), channel_id=1, replica_groups=mesh['xh'=4,'zh'=2,'quad'=4,'xl'=2,'y'=8,'c'=2] {'c'}, dimensions={0}, use_global_device_ids=true | all-gather | bytes 196608 | tf_op jit(solution)/shard_map/all_gather | solution.py:50
  32.8 14.0 %all-gather = bf16[8,1,4,8,4,128]{5,3,4,2,1,0:T(8,128)(2,1)S(1)} all-gather(bf16[2,1,4,8,4,128]{5,3,4,2,1,0:T(8,128)(2,1)S(1)} %constant_dynamic-slice_fusion.1), channel_id=2, replica_groups=mesh['xh'=4,'zh'=2,'quad'=4,'xl'=2,'y'=8,'c'=2] {'quad'}, dimensions={0}, use_global_device_ids=true | all-gather | bytes 327680 | tf_op jit(solution)/shard_map/all_gather | solution.py:52
  46.8 12.9 %all_gather.27 = bf16[2,2,8,16,128]{4,3,2,1,0:T(8,128)(2,1)S(1)} all-gather(bf16[1,2,8,16,128]{4,3,2,1,0:T(8,128)(2,1)S(1)} %copy.68), channel_id=1, replica_groups=mesh['xh'=4,'zh'=2,'quad'=4,'xl'=2,'y'=8,'c'=2] {'zh'}, dimensions={0}, use_global_device_ids=true | all-gather | bytes 196608 | tf_op jit(solution)/shard_map/all_gather | solution.py:55
  59.7 16.1 %all-gather.1 = bf16[8,2,8,16,128]{4,3,2,1,0:T(8,128)(2,1)S(1)} all-gather(bf16[2,2,8,16,128]{4,3,2,1,0:T(8,128)(2,1)S(1)} %all_gather.27), channel_id=3, replica_groups=mesh['xh'=4,'zh'=2,'quad'=4,'xl'=2,'y'=8,'c'=2] {'xh'}, dimensions={0}, use_global_device_ids=true | all-gather | bytes 655360 | tf_op jit(solution)/shard_map/all_gather | solution.py:56
  75.8 4.3 %all-to-all-done.1 = bf16[8,8,64,256]{3,2,1,0:T(8,128)(2,1)S(1)} async-done(((bf16[8,8,64,256]{3,2,1,0:T(8,128)(2,1)}), bf16[8,8,64,256]{3,2,1,0:T(8,128)(2,1)S(1)}, u32[]{:S(2)}, u32[]{:S(2)}) %all-to-all-start.1) | async-done | bytes 2097184 | tf_op jit(solution)/shard_map/all_to_all | solution.py:44
  80.0 0.4 fusion.30
  80.5 1.9 %collective-permute-start = (f32[4,8,16,256]{3,2,1,0:T(8,128)S(1)}, f32[4,8,16,256]{3,2,1,0:T(8,128)S(1)}, u32[]{:S(2)}, u32[]{:S(2)}) collective-permute-start(f32[4,8,16,256]{3,2,1,0:T(8,128)S(1)} %fusion.30), channel_id=1, source_target_pairs={{0,1},{1,0},{2,3},{3,2},{4,5},{5,4},{6,7},{7,6},{8,9},{9,8},{10,11... | collective-permute-start | bytes 1572872 | tf_op jit(solution)/shard_map/ppermute | solution.py:61
  82.4 1.9 %collective-permute-done = f32[4,8,16,256]{3,2,1,0:T(8,128)S(1)} collective-permute-done((f32[4,8,16,256]{3,2,1,0:T(8,128)S(1)}, f32[4,8,16,256]{3,2,1,0:T(8,128)S(1)}, u32[]{:S(2)}, u32[]{:S(2)}) %collective-permute-start) | collective-permute-done | bytes 524320 | tf_op jit(solution)/shard_map/ppermute | solution.py:61
  84.3 0.5 fusion.36
  84.8 0.0 copy-start.2
  84.9 0.0 copy-start.3
  84.9 0.8 pad_maximum_fusion
  85.7 4.1 %all-to-all-start.2 = ((bf16[4,128,384]{2,1,0:T(8,128)(2,1)}), bf16[4,128,384]{2,1,0:T(8,128)(2,1)S(1)}, u32[]{:S(2)}, u32[]{:S(2)}) async-start(bf16[4,128,384]{2,1,0:T(8,128)(2,1)} %pad_maximum_fusion), calls=%async_computation.2 | async-start | bytes 786432 | tf_op jit(solution)/shard_map/all_to_all | solution.py:67
  89.7 0.4 copy.107
  91.4 0.0 copy-done.3
  91.4 0.4 copy.104
  91.8 0.0 copy-done
  91.8 0.0 copy-start.9
  91.9 9.9 %all-to-all-done.2 = bf16[4,128,384]{2,1,0:T(8,128)(2,1)S(1)} async-done(((bf16[4,128,384]{2,1,0:T(8,128)(2,1)}), bf16[4,128,384]{2,1,0:T(8,128)(2,1)S(1)}, u32[]{:S(2)}, u32[]{:S(2)}) %all-to-all-start.2) | async-done | bytes 393248 | tf_op jit(solution)/shard_map/all_to_all | solution.py:67
  101.7 0.1 convert_reduce_fusion.2
  101.8 0.1 copy.109
  101.9 0.1 copy.110
  102.0 0.5 bitcast_reduce_fusion
  102.6 0.2 fusion.57
  102.8 0.0 copy-start.4
  102.8 0.1 copy.108
  102.9 0.0 copy-start.7
  102.9 0.4 fusion.45
  103.4 0.0 copy-done.9
  103.4 0.2 copy-done.7
  103.6 0.6 fusion.11
  104.1 0.0 copy-start.12
  104.1 0.0 copy-start.14
  104.2 0.6 fusion.19
  104.8 0.0 copy-done.14
  104.8 0.9 multiply_reduce_fusion
  105.8 0.1 copy.82
  106.0 10.8 %all_to_all.31 = bf16[4,128,256]{2,1,0:T(8,128)(2,1)S(1)} all-to-all(bf16[4,128,256]{2,1,0:T(8,128)(2,1)S(1)} %broadcast_in_dim.81), channel_id=1, replica_groups=mesh['xh'=4,'zh'=2,'quad'=4,'xl'=2,'y'=8,'c'=2] {'quad'}, dimensions={0} | all-to-all | bytes 524288 | tf_op jit(solution)/shard_map/all_to_all | solution.py:82
  116.8 2.2 %all-gather.2 = bf16[8,128,256]{2,1,0:T(8,128)(2,1)S(1)} all-gather(bf16[4,128,256]{2,1,0:T(8,128)(2,1)S(1)} %all_to_all.31), channel_id=4, replica_groups=mesh['xh'=4,'zh'=2,'quad'=4,'xl'=2,'y'=8,'c'=2] {'c'}, dimensions={0}, use_global_device_ids=true | all-gather | bytes 786432 | tf_op jit(solution)/shard_map/all_gather | solution.py:83
  119.0 2.3 %fusion.29 = bf16[8,2,8,16,128]{4,3,0,1,2:T(8,128)(2,1)S(1)} fusion(bf16[8,4,128,256,1,1]{3,2,1,5,4,0:T(8,128)(2,1)} %bitcast.172, bf16[2,4,8,16,256]{4,3,2,1,0:T(8,128)(2,1)S(1)} %bitcast.178), kind=kOutput, calls=%fused_computation.37 | convolution fusion | flops 537133056 | bytes 3145728 | tf_op jit(solution)/shard_map/shzrn,yhdn->zsyrd/dot_general | solution.py:86
  121.3 0.0 copy-start.5
  121.3 0.0 copy-start.8
  121.3 0.8 copy.84
  122.2 15.2 %all-to-all-start.4 = ((bf16[8,2,8,16,128]{4,3,1,2,0:T(8,128)(2,1)}), bf16[8,2,8,16,128]{4,3,1,2,0:T(8,128)(2,1)S(1)}, u32[]{:S(2)}, u32[]{:S(2)}) async-start(bf16[8,2,8,16,128]{4,3,1,2,0:T(8,128)(2,1)} %copy.84), calls=%async_computation.4 | async-start | bytes 1048576 | tf_op jit(solution)/shard_map/all_to_all | solution.py:87
  137.4 1.3 fusion.80
  138.7 1.4 copy.77
  140.2 17.7 %all-to-all-done.4 = bf16[8,2,8,16,128]{4,3,1,2,0:T(8,128)(2,1)S(1)} async-done(((bf16[8,2,8,16,128]{4,3,1,2,0:T(8,128)(2,1)}), bf16[8,2,8,16,128]{4,3,1,2,0:T(8,128)(2,1)S(1)}, u32[]{:S(2)}, u32[]{:S(2)}) %all-to-all-start.4) | async-done | bytes 524320 | tf_op jit(solution)/shard_map/all_to_all | solution.py:87
  157.9 0.1 convert_reduce_fusion.1
  157.9 0.1 copy.86
  158.0 0.7 copy.87
  158.7 3.4 %all-to-all-start.5 = ((f32[8,8,4,128]{3,1,2,0:T(8,128)}), f32[8,8,4,128]{3,1,2,0:T(8,128)S(1)}, u32[]{:S(2)}, u32[]{:S(2)}) async-start(f32[8,8,4,128]{3,1,2,0:T(8,128)} %bitcast.50), calls=%async_computation.5 | async-start | bytes 262144 | tf_op jit(solution)/shard_map/all_to_all | solution.py:91
  162.1 1.1 select_convert_fusion
  163.2 5.6 %all-to-all-done.5 = f32[8,8,4,128]{3,1,2,0:T(8,128)S(1)} async-done(((f32[8,8,4,128]{3,1,2,0:T(8,128)}), f32[8,8,4,128]{3,1,2,0:T(8,128)S(1)}, u32[]{:S(2)}, u32[]{:S(2)}) %all-to-all-start.5) | async-done | bytes 131104 | tf_op jit(solution)/shard_map/all_to_all | solution.py:91
  168.7 0.2 reshape.141
  168.9 0.2 copy.88
  169.1 0.9 reshape.142
  (36 shorter events, 0.3 us)
Async XLA Ops:
  0.6 91.2 %copy-start = (f32[8,128]{1,0:T(8,128)S(1)}, f32[8,128]{1,0:T(8,128)}, u32[]{:S(2)}) copy-start(f32[8,128]{1,0:T(8,128)} %param.12) | copy-start | bytes 12292
  25.5 4.9 %copy-start.6 = (bf16[1,4,8192]{2,1,0:T(4,128)(2,1)S(1)}, bf16[1,4,8192]{2,1,0:T(4,128)(2,1)}, u32[]{:S(2)}) copy-start(bf16[1,4,8192]{2,1,0:T(4,128)(2,1)} %param.9) | copy-start | bytes 196612
  25.5 54.5 %all-to-all-start.1 = ((bf16[8,8,64,256]{3,2,1,0:T(8,128)(2,1)}), bf16[8,8,64,256]{3,2,1,0:T(8,128)(2,1)S(1)}, u32[]{:S(2)}, u32[]{:S(2)}) async-start(bf16[8,8,64,256]{3,2,1,0:T(8,128)(2,1)} %broadcast_in_dim.70), calls=%async_computation.1 | async-start | bytes 4194304 | tf_op jit(solution)/shard_map/all_to_all | solution.py:44
  80.0 4.3 %copy-start.1 = (bf16[8,8,64,256]{3,2,1,0:T(8,128)(2,1)}, bf16[8,8,64,256]{3,2,1,0:T(8,128)(2,1)S(1)}, u32[]{:S(2)}) copy-start(bf16[8,8,64,256]{3,2,1,0:T(8,128)(2,1)S(1)} %all-to-all-done.1) | copy-start | bytes 6291460
  80.5 3.8 %collective-permute-start = (f32[4,8,16,256]{3,2,1,0:T(8,128)S(1)}, f32[4,8,16,256]{3,2,1,0:T(8,128)S(1)}, u32[]{:S(2)}, u32[]{:S(2)}) collective-permute-start(f32[4,8,16,256]{3,2,1,0:T(8,128)S(1)} %fusion.30), channel_id=1, source_target_pairs={{0,1},{1,0},{2,3},{3,2},{4,5},{5,4},{6,7},{7,6},{8,9},{9,8},{10,11... | collective-permute-start | bytes 1572872 | tf_op jit(solution)/shard_map/ppermute | solution.py:61
  84.8 5.0 %copy-start.2 = (bf16[1,384,1024]{2,1,0:T(8,128)(2,1)S(1)}, bf16[1,384,1024]{2,1,0:T(8,128)(2,1)}, u32[]{:S(2)}) copy-start(bf16[1,384,1024]{2,1,0:T(8,128)(2,1)} %param.8) | copy-start | bytes 2359300
  84.9 6.5 %copy-start.3 = (bf16[1,384,1024]{2,1,0:T(8,128)(2,1)S(1)}, bf16[1,384,1024]{2,1,0:T(8,128)(2,1)}, u32[]{:S(2)}) copy-start(bf16[1,384,1024]{2,1,0:T(8,128)(2,1)} %param.13) | copy-start | bytes 2359300
  85.7 16.0 %all-to-all-start.2 = ((bf16[4,128,384]{2,1,0:T(8,128)(2,1)}), bf16[4,128,384]{2,1,0:T(8,128)(2,1)S(1)}, u32[]{:S(2)}, u32[]{:S(2)}) async-start(bf16[4,128,384]{2,1,0:T(8,128)(2,1)} %pad_maximum_fusion), calls=%async_computation.2 | async-start | bytes 786432 | tf_op jit(solution)/shard_map/all_to_all | solution.py:67
  91.8 10.7 %copy-start.11 = (pred[128]{0:T(512)(128)(4,1)}, pred[128]{0:T(512)(128)(4,1)S(1)}, u32[]{:S(2)}) copy-start(pred[128]{0:T(512)(128)(4,1)S(1)} %iota_compare_fusion.1) | copy-start | bytes 388
  91.8 11.6 %copy-start.9 = (pred[384]{0:T(512)(128)(4,1)}, pred[384]{0:T(512)(128)(4,1)S(1)}, u32[]{:S(2)}) copy-start(pred[384]{0:T(512)(128)(4,1)S(1)} %iota_compare_fusion) | copy-start | bytes 1156
  91.8 10.7 %copy-start.13 = (f32[128]{0:T(128)}, f32[128]{0:T(128)S(1)}, u32[]{:S(2)}) copy-start(f32[128]{0:T(128)S(1)} %fusion.88) | copy-start | bytes 1540
  102.8 2.0 %copy-start.4 = (f32[8,384]{1,0:T(8,128)}, f32[8,384]{1,0:T(8,128)S(1)}, u32[]{:S(2)}) copy-start(f32[8,384]{1,0:T(8,128)S(1)} %fusion.57) | copy-start | bytes 36868
  102.9 0.6 copy-start.7
  104.1 0.7 copy-start.12
  104.1 0.7 copy-start.14
  121.3 16.1 %copy-start.5 = (f32[8,384]{1,0:T(8,128)S(1)}, f32[8,384]{1,0:T(8,128)}, u32[]{:S(2)}) copy-start(f32[8,384]{1,0:T(8,128)} %copy-done.4) | copy-start | bytes 36868
  121.3 16.1 %copy-start.8 = (bf16[128,128]{0,1:T(8,128)(2,1)S(1)}, bf16[128,128]{0,1:T(8,128)(2,1)}, u32[]{:S(2)}) copy-start(bf16[128,128]{0,1:T(8,128)(2,1)} %copy-done.7) | copy-start | bytes 98308
  122.2 35.7 %all-to-all-start.4 = ((bf16[8,2,8,16,128]{4,3,1,2,0:T(8,128)(2,1)}), bf16[8,2,8,16,128]{4,3,1,2,0:T(8,128)(2,1)S(1)}, u32[]{:S(2)}, u32[]{:S(2)}) async-start(bf16[8,2,8,16,128]{4,3,1,2,0:T(8,128)(2,1)} %copy.84), calls=%async_computation.4 | async-start | bytes 1048576 | tf_op jit(solution)/shard_map/all_to_all | solution.py:87
  138.7 23.3 %copy-start.10 = (pred[384]{0:T(512)(128)(4,1)S(1)}, pred[384]{0:T(512)(128)(4,1)}, u32[]{:S(2)}) copy-start(pred[384]{0:T(512)(128)(4,1)} %copy-done.9) | copy-start | bytes 1156
  158.7 10.1 %all-to-all-start.5 = ((f32[8,8,4,128]{3,1,2,0:T(8,128)}), f32[8,8,4,128]{3,1,2,0:T(8,128)S(1)}, u32[]{:S(2)}, u32[]{:S(2)}) async-start(f32[8,8,4,128]{3,1,2,0:T(8,128)} %bitcast.50), calls=%async_computation.5 | async-start | bytes 262144 | tf_op jit(solution)/shard_map/all_to_all | solution.py:91

commit v3 on v2

--- a/solution.py
+++ b/solution.py
@@ -84,11 +84,14 @@
 
     d_both = d_both.reshape(2, QUAD, nrest, QUAD * rows, 2 * head)
     term = jnp.einsum("shzrn,yhdn->zsyrd", d_both, weight, preferred_element_type=jnp.float32)
-    term = lax.all_to_all(term.astype(jnp.bfloat16), REST, 0, 0)
-    total = jnp.sum(term.astype(jnp.float32), axis=0)
-    total = total.reshape(2, ny, QUAD, rows, wide).transpose(2, 0, 1, 3, 4)
-    total = total.reshape(QUAD * 2, ny, rows, wide)
-    grads = lax.all_to_all(total, ("quad", "c"), 0, 0)
+    term = term.astype(jnp.bfloat16).reshape((nrest // 2, 2) + term.shape[1:])
+    term = lax.all_to_all(term, "xh", 0, 0)
+    total = jnp.sum(term.astype(jnp.float32), axis=0).astype(jnp.bfloat16)
+    total = total.reshape(2, 2, ny, QUAD, rows, wide).transpose(0, 3, 1, 2, 4, 5)
+    total = total.reshape(2 * QUAD * 2, ny, rows, wide)
+    grads = lax.all_to_all(total, ("zh", "quad", "c"), 0, 0)
+    grads = grads.reshape(2, QUAD, 2, ny, rows, wide)
+    grads = grads[0].astype(jnp.float32) + grads[1].astype(jnp.float32)
     grads = grads.reshape(QUAD, 2, ny, rows, 2, unit).transpose(3, 4, 2, 1, 0, 5)
     return mixed.astype(jnp.bfloat16)[None], grads.reshape(1, rows, model)
 

time: 171 us -> 168 us (0.982)
  the two profiles are of different devices: /device:TPU:2 before, /device:TPU:3 now
where the time goes in v3:
time: 168 us
  blocking collectives  74.2 us (44%)
  waiting for transfers between devices  39 us (23%)
  starting transfers between devices  33.2 us (20%)
  local copies, waits for them, and re-layouts  7.75 us (5%)
  matrix products  6.93 us (4%)
  other arithmetic  3.95 us (2%)
  between operations  2.4 us (1%)
    all_to_all x1, blocking collectives, local(): near = lax.all_to_all(own, ('quad', 'xl'), 0, 0)  16.6 us
    all_gather x1, blocking collectives, local(): image = lax.all_gather(pieces, 'xh', axis=0)  15.8 us
    all_to_all x1, waiting for transfers between devices, local(): term = lax.all_to_all(term, 'xh', 0, 0)  13.1 us
    all_to_all x1, starting transfers between devices, local(): grads = lax.all_to_all(total, ('zh', 'quad', 'c'), 0, 0)  12.7 us
    all_gather x1, blocking collectives, local(): pieces = lax.all_gather(pieces, 'zh', axis=0)  12 us
    all_gather x1, blocking collectives, local(): pieces = lax.all_gather(pieces, 'quad', axis=0)  11.8 us
    all_to_all x1, waiting for transfers between devices, local(): part = lax.all_to_all(part.astype(jnp.bfloat16), 'quad', 0, 0)  9.12 us
    all_to_all x1, starting transfers between devices, local(): lax.all_to_all(jnp.broadcast_to(near[None], (ny,) + near.shape), 'y', 0, 0)  8.81 us
  transfers between devices with their start and end apart: 5, of which 5 were waited for; matrix products, arithmetic and copies ran while one was open for 3% of the time, Pallas kernels for 0%

profile of v3, /device:TPU:3, one launch (start us, length us, event | category | flops | bytes accessed | tf_op | source)
XLA Modules:
  0.0 167.5 jit_solution(16253620346831755224)
XLA Ops:
  0.6 0.0 copy-start
  0.6 0.9 maximum_bitcast_fusion
  1.6 16.6 %all_to_all.30 = bf16[8,64,256]{2,1,0:T(8,128)(2,1)S(1)} all-to-all(bf16[8,64,256]{2,1,0:T(8,128)(2,1)S(1)} %bitcast.172), channel_id=1, replica_groups=mesh['xh'=4,'zh'=2,'quad'=4,'xl'=2,'y'=8,'c'=2] {'quad','xl'}, dimensions={0} | all-to-all | bytes 524288 | tf_op jit(solution)/shard_map/all_to_all | solution.py:43
  18.2 1.6 broadcast_in_dim.70
  19.8 8.8 %all-to-all-start.1 = ((bf16[8,8,64,256]{3,2,1,0:T(8,128)(2,1)}), bf16[8,8,64,256]{3,2,1,0:T(8,128)(2,1)S(1)}, u32[]{:S(2)}, u32[]{:S(2)}) async-start(bf16[8,8,64,256]{3,2,1,0:T(8,128)(2,1)} %broadcast_in_dim.70), calls=%async_computation.1 | async-start | bytes 4194304 | tf_op jit(solution)/shard_map/all_to_all | solution.py:44
  28.6 0.2 reshape_squeeze.3
  28.7 0.1 copy.126
  28.9 0.1 all_gather_reshape.6
  29.0 4.1 %all_gather.24 = bf16[2,2,4,8,4,128]{5,3,4,2,1,0:T(8,128)(2,1)S(1)} all-gather(bf16[1,2,4,8,4,128]{5,3,4,2,1,0:T(8,128)(2,1)S(1)} %all_gather_reshape.6), channel_id=1, replica_groups=mesh['xh'=4,'zh'=2,'quad'=4,'xl'=2,'y'=8,'c'=2] {'c'}, dimensions={0}, use_global_device_ids=true | all-gather | bytes 196608 | tf_op jit(solution)/shard_map/all_gather | solution.py:50
  33.1 11.8 %all-gather = bf16[8,1,4,8,4,128]{5,3,4,2,1,0:T(8,128)(2,1)S(1)} all-gather(bf16[2,1,4,8,4,128]{5,3,4,2,1,0:T(8,128)(2,1)S(1)} %constant_dynamic-slice_fusion.1), channel_id=2, replica_groups=mesh['xh'=4,'zh'=2,'quad'=4,'xl'=2,'y'=8,'c'=2] {'quad'}, dimensions={0}, use_global_device_ids=true | all-gather | bytes 327680 | tf_op jit(solution)/shard_map/all_gather | solution.py:52
  44.9 12.0 %all_gather.27 = bf16[2,2,8,16,128]{4,3,2,1,0:T(8,128)(2,1)S(1)} all-gather(bf16[1,2,8,16,128]{4,3,2,1,0:T(8,128)(2,1)S(1)} %copy.68), channel_id=1, replica_groups=mesh['xh'=4,'zh'=2,'quad'=4,'xl'=2,'y'=8,'c'=2] {'zh'}, dimensions={0}, use_global_device_ids=true | all-gather | bytes 196608 | tf_op jit(solution)/shard_map/all_gather | solution.py:55
  56.9 15.8 %all-gather.1 = bf16[8,2,8,16,128]{4,3,2,1,0:T(8,128)(2,1)S(1)} all-gather(bf16[2,2,8,16,128]{4,3,2,1,0:T(8,128)(2,1)S(1)} %all_gather.27), channel_id=3, replica_groups=mesh['xh'=4,'zh'=2,'quad'=4,'xl'=2,'y'=8,'c'=2] {'xh'}, dimensions={0}, use_global_device_ids=true | all-gather | bytes 655360 | tf_op jit(solution)/shard_map/all_gather | solution.py:56
  72.7 7.5 %all-to-all-done.1 = bf16[8,8,64,256]{3,2,1,0:T(8,128)(2,1)S(1)} async-done(((bf16[8,8,64,256]{3,2,1,0:T(8,128)(2,1)}), bf16[8,8,64,256]{3,2,1,0:T(8,128)(2,1)S(1)}, u32[]{:S(2)}, u32[]{:S(2)}) %all-to-all-start.1) | async-done | bytes 2097184 | tf_op jit(solution)/shard_map/all_to_all | solution.py:44
  80.2 0.4 fusion.29
  80.7 2.4 %collective-permute-start = (f32[4,8,16,256]{3,2,1,0:T(8,128)S(1)}, f32[4,8,16,256]{3,2,1,0:T(8,128)S(1)}, u32[]{:S(2)}, u32[]{:S(2)}) collective-permute-start(f32[4,8,16,256]{3,2,1,0:T(8,128)S(1)} %fusion.29), channel_id=1, source_target_pairs={{0,1},{1,0},{2,3},{3,2},{4,5},{5,4},{6,7},{7,6},{8,9},{9,8},{10,11... | collective-permute-start | bytes 1572872 | tf_op jit(solution)/shard_map/ppermute | solution.py:61
  83.1 1.5 collective-permute-done
  84.6 0.4 fusion.35
  85.1 0.0 copy-start.2
  85.1 0.0 copy-start.3
  85.2 0.8 pad_maximum_fusion
  86.0 3.8 %all-to-all-start.2 = ((bf16[4,128,384]{2,1,0:T(8,128)(2,1)}), bf16[4,128,384]{2,1,0:T(8,128)(2,1)S(1)}, u32[]{:S(2)}, u32[]{:S(2)}) async-start(bf16[4,128,384]{2,1,0:T(8,128)(2,1)} %pad_maximum_fusion), calls=%async_computation.2 | async-start | bytes 786432 | tf_op jit(solution)/shard_map/all_to_all | solution.py:67
  89.7 0.0 copy-done.2
  89.7 0.4 copy.107
  91.4 0.4 copy.104
  91.8 0.0 copy-start.11
  91.9 0.0 copy-start.13
  91.9 9.1 %all-to-all-done.2 = bf16[4,128,384]{2,1,0:T(8,128)(2,1)S(1)} async-done(((bf16[4,128,384]{2,1,0:T(8,128)(2,1)}), bf16[4,128,384]{2,1,0:T(8,128)(2,1)S(1)}, u32[]{:S(2)}, u32[]{:S(2)}) %all-to-all-start.2) | async-done | bytes 393248 | tf_op jit(solution)/shard_map/all_to_all | solution.py:67
  101.0 0.1 convert_reduce_fusion.1
  101.1 0.1 copy.109
  101.2 0.1 copy.110
  101.3 0.5 bitcast_reduce_fusion
  101.8 0.2 fusion.56
  102.1 0.0 copy-start.4
  102.1 0.1 copy.108
  102.2 0.0 copy-start.7
  102.2 0.4 fusion.44
  102.7 0.2 copy-done.7
  102.8 0.6 fusion.11
  103.4 0.6 fusion.19
  104.1 0.0 copy-done.4
  104.1 0.0 copy-done.12
  104.1 0.0 copy-done.14
  104.1 0.9 multiply_reduce_fusion
  105.1 0.1 copy.82
  105.3 8.5 %all_to_all.31 = bf16[4,128,256]{2,1,0:T(8,128)(2,1)S(1)} all-to-all(bf16[4,128,256]{2,1,0:T(8,128)(2,1)S(1)} %broadcast_in_dim.81), channel_id=1, replica_groups=mesh['xh'=4,'zh'=2,'quad'=4,'xl'=2,'y'=8,'c'=2] {'quad'}, dimensions={0} | all-to-all | bytes 524288 | tf_op jit(solution)/shard_map/all_to_all | solution.py:82
  113.8 5.5 %all-gather.2 = bf16[8,128,256]{2,1,0:T(8,128)(2,1)S(1)} all-gather(bf16[4,128,256]{2,1,0:T(8,128)(2,1)S(1)} %all_to_all.31), channel_id=4, replica_groups=mesh['xh'=4,'zh'=2,'quad'=4,'xl'=2,'y'=8,'c'=2] {'c'}, dimensions={0}, use_global_device_ids=true | all-gather | bytes 786432 | tf_op jit(solution)/shard_map/all_gather | solution.py:83
  119.3 2.3 %fusion.28 = bf16[8,128,2,8,16]{1,4,3,2,0:T(8,128)(2,1)S(1)} fusion(bf16[8,4,128,256,1,1]{3,2,1,5,4,0:T(8,128)(2,1)} %bitcast.171, bf16[2,4,8,16,256]{4,3,2,1,0:T(8,128)(2,1)S(1)} %bitcast.177), kind=kOutput, calls=%fused_computation.36 | convolution fusion | flops 537133056 | bytes 3145728 | tf_op jit(solution)/shard_map/shzrn,yhdn->zsyrd/dot_general | solution.py:86
  121.6 0.0 copy-start.5
  121.6 0.0 copy-start.8
  121.6 0.9 copy.84
  122.5 5.6 %all-to-all-start.4 = ((bf16[4,2,2,8,16,128]{5,4,1,2,3,0:T(8,128)(2,1)}), bf16[4,2,2,8,16,128]{5,4,1,2,3,0:T(8,128)(2,1)S(1)}, u32[]{:S(2)}, u32[]{:S(2)}) async-start(bf16[4,2,2,8,16,128]{5,4,1,2,3,0:T(8,128)(2,1)} %copy.84), calls=%async_computation.4 | async-start | bytes 1048576 | tf_op jit(solution)/shard_map/all_to_all | solution.py:88
  128.1 1.3 fusion.79
  129.4 1.4 copy.77
  130.8 13.1 %all-to-all-done.4 = bf16[4,2,2,8,16,128]{5,4,1,2,3,0:T(8,128)(2,1)S(1)} async-done(((bf16[4,2,2,8,16,128]{5,4,1,2,3,0:T(8,128)(2,1)}), bf16[4,2,2,8,16,128]{5,4,1,2,3,0:T(8,128)(2,1)S(1)}, u32[]{:S(2)}, u32[]{:S(2)}) %all-to-all-start.4) | async-done | bytes 524320 | tf_op jit(solution)/shard_map/all_to_all | solution.py:88
  143.9 0.1 reduce_sum.94
  144.0 0.1 copy.86
  144.1 0.7 copy.87
  144.7 12.7 %all-to-all-start.5 = ((bf16[16,8,4,128]{3,1,2,0:T(8,128)(2,1)}), bf16[16,8,4,128]{3,1,2,0:T(8,128)(2,1)S(1)}, u32[]{:S(2)}, u32[]{:S(2)}) async-start(bf16[16,8,4,128]{3,1,2,0:T(8,128)(2,1)} %bitcast.51), calls=%async_computation.5 | async-start | bytes 262144 | tf_op jit(solution)/shard_map/all_to_all | solution.py:92
  157.4 0.0 copy-done.10
  157.4 1.1 select_convert_fusion
  158.5 7.8 %all-to-all-done.5 = bf16[16,8,4,128]{3,1,2,0:T(8,128)(2,1)S(1)} async-done(((bf16[16,8,4,128]{3,1,2,0:T(8,128)(2,1)}), bf16[16,8,4,128]{3,1,2,0:T(8,128)(2,1)S(1)}, u32[]{:S(2)}, u32[]{:S(2)}) %all-to-all-start.5) | async-done | bytes 131104 | tf_op jit(solution)/shard_map/all_to_all | solution.py:92
  166.3 0.2 add.62
  166.5 0.2 copy.88
  166.7 0.9 reshape.153
  (37 shorter events, 0.3 us)
Async XLA Ops:
  0.6 91.2 %copy-start = (f32[8,128]{1,0:T(8,128)S(1)}, f32[8,128]{1,0:T(8,128)}, u32[]{:S(2)}) copy-start(f32[8,128]{1,0:T(8,128)} %param.12) | copy-start | bytes 12292
  19.8 8.8 %copy-start.6 = (bf16[1,4,8192]{2,1,0:T(4,128)(2,1)S(1)}, bf16[1,4,8192]{2,1,0:T(4,128)(2,1)}, u32[]{:S(2)}) copy-start(bf16[1,4,8192]{2,1,0:T(4,128)(2,1)} %param.9) | copy-start | bytes 196612
  19.8 60.5 %all-to-all-start.1 = ((bf16[8,8,64,256]{3,2,1,0:T(8,128)(2,1)}), bf16[8,8,64,256]{3,2,1,0:T(8,128)(2,1)S(1)}, u32[]{:S(2)}, u32[]{:S(2)}) async-start(bf16[8,8,64,256]{3,2,1,0:T(8,128)(2,1)} %broadcast_in_dim.70), calls=%async_computation.1 | async-start | bytes 4194304 | tf_op jit(solution)/shard_map/all_to_all | solution.py:44
  80.2 4.4 %copy-start.1 = (bf16[8,8,64,256]{3,2,1,0:T(8,128)(2,1)}, bf16[8,8,64,256]{3,2,1,0:T(8,128)(2,1)S(1)}, u32[]{:S(2)}) copy-start(bf16[8,8,64,256]{3,2,1,0:T(8,128)(2,1)S(1)} %all-to-all-done.1) | copy-start | bytes 6291460
  80.7 3.9 %collective-permute-start = (f32[4,8,16,256]{3,2,1,0:T(8,128)S(1)}, f32[4,8,16,256]{3,2,1,0:T(8,128)S(1)}, u32[]{:S(2)}, u32[]{:S(2)}) collective-permute-start(f32[4,8,16,256]{3,2,1,0:T(8,128)S(1)} %fusion.29), channel_id=1, source_target_pairs={{0,1},{1,0},{2,3},{3,2},{4,5},{5,4},{6,7},{7,6},{8,9},{9,8},{10,11... | collective-permute-start | bytes 1572872 | tf_op jit(solution)/shard_map/ppermute | solution.py:61
  85.1 4.7 %copy-start.2 = (bf16[1,384,1024]{2,1,0:T(8,128)(2,1)S(1)}, bf16[1,384,1024]{2,1,0:T(8,128)(2,1)}, u32[]{:S(2)}) copy-start(bf16[1,384,1024]{2,1,0:T(8,128)(2,1)} %param.8) | copy-start | bytes 2359300
  85.1 6.3 %copy-start.3 = (bf16[1,384,1024]{2,1,0:T(8,128)(2,1)S(1)}, bf16[1,384,1024]{2,1,0:T(8,128)(2,1)}, u32[]{:S(2)}) copy-start(bf16[1,384,1024]{2,1,0:T(8,128)(2,1)} %param.13) | copy-start | bytes 2359300
  86.0 15.0 %all-to-all-start.2 = ((bf16[4,128,384]{2,1,0:T(8,128)(2,1)}), bf16[4,128,384]{2,1,0:T(8,128)(2,1)S(1)}, u32[]{:S(2)}, u32[]{:S(2)}) async-start(bf16[4,128,384]{2,1,0:T(8,128)(2,1)} %pad_maximum_fusion), calls=%async_computation.2 | async-start | bytes 786432 | tf_op jit(solution)/shard_map/all_to_all | solution.py:67
  91.8 10.0 %copy-start.11 = (pred[128]{0:T(512)(128)(4,1)}, pred[128]{0:T(512)(128)(4,1)S(1)}, u32[]{:S(2)}) copy-start(pred[128]{0:T(512)(128)(4,1)S(1)} %iota_compare_fusion.1) | copy-start | bytes 388
  91.8 10.8 %copy-start.9 = (pred[384]{0:T(512)(128)(4,1)}, pred[384]{0:T(512)(128)(4,1)S(1)}, u32[]{:S(2)}) copy-start(pred[384]{0:T(512)(128)(4,1)S(1)} %iota_compare_fusion) | copy-start | bytes 1156
  91.9 10.0 %copy-start.13 = (f32[128]{0:T(128)}, f32[128]{0:T(128)S(1)}, u32[]{:S(2)}) copy-start(f32[128]{0:T(128)S(1)} %fusion.87) | copy-start | bytes 1540
  102.1 2.0 %copy-start.4 = (f32[8,384]{1,0:T(8,128)}, f32[8,384]{1,0:T(8,128)S(1)}, u32[]{:S(2)}) copy-start(f32[8,384]{1,0:T(8,128)S(1)} %fusion.56) | copy-start | bytes 36868
  102.2 0.6 copy-start.7
  103.4 0.7 copy-start.12
  103.4 0.7 copy-start.14
  121.6 6.5 %copy-start.5 = (f32[8,384]{1,0:T(8,128)S(1)}, f32[8,384]{1,0:T(8,128)}, u32[]{:S(2)}) copy-start(f32[8,384]{1,0:T(8,128)} %copy-done.4) | copy-start | bytes 36868
  121.6 6.4 %copy-start.8 = (bf16[128,128]{0,1:T(8,128)(2,1)S(1)}, bf16[128,128]{0,1:T(8,128)(2,1)}, u32[]{:S(2)}) copy-start(bf16[128,128]{0,1:T(8,128)(2,1)} %copy-done.7) | copy-start | bytes 98308
  122.5 21.4 %all-to-all-start.4 = ((bf16[4,2,2,8,16,128]{5,4,1,2,3,0:T(8,128)(2,1)}), bf16[4,2,2,8,16,128]{5,4,1,2,3,0:T(8,128)(2,1)S(1)}, u32[]{:S(2)}, u32[]{:S(2)}) async-start(bf16[4,2,2,8,16,128]{5,4,1,2,3,0:T(8,128)(2,1)} %copy.84), calls=%async_computation.4 | async-start | bytes 1048576 | tf_op jit(solution)/shard_map/all_to_all | solution.py:88
  129.4 28.0 %copy-start.10 = (pred[384]{0:T(512)(128)(4,1)S(1)}, pred[384]{0:T(512)(128)(4,1)}, u32[]{:S(2)}) copy-start(pred[384]{0:T(512)(128)(4,1)} %copy-done.9) | copy-start | bytes 1156
  144.7 21.6 %all-to-all-start.5 = ((bf16[16,8,4,128]{3,1,2,0:T(8,128)(2,1)}), bf16[16,8,4,128]{3,1,2,0:T(8,128)(2,1)S(1)}, u32[]{:S(2)}, u32[]{:S(2)}) async-start(bf16[16,8,4,128]{3,1,2,0:T(8,128)(2,1)} %bitcast.51), calls=%async_computation.5 | async-start | bytes 262144 | tf_op jit(solution)/shard_map/all_to_all | solution.py:92
